TPU v7x, 32 devices: a whole 2x2x4 slice. The times are simulated.
32 devices in a mesh: req: 16 (over z, y, x), tp: 2 (over core).
Axes of the slice: x: 2, y: 2, z: 4, core: 2. Of those that a mesh axis runs over, the one named last changes fastest.
Arguments:
- hidden: bfloat16 [16, 32, 2048], P('req', 'tp'), may hold values from -4.5 to 4.5
- norm_gain: float32 [2048], replicated, may hold values from 0.1 to 1.9
- embedding: bfloat16 [16384, 2048], P(('req', 'tp')), may hold values from -0.79549513 to 0.79549513
- target_ids: int32 [16, 32], P('req', 'tp'), may hold values from 0 to 16383
- lengths: int32 [16], P('req'), may hold values from 1 to 32, 320 in all
- response_mask: int32 [16, 32], P('req', 'tp'), may hold values 0 or 1
Outputs:
- logprob: float32 [16, 32], P('req', 'tp')
- entropy: float32 [16, 32], P('req', 'tp')
All inputs are finite; a program needn't handle non-finite values. No bound on the sum of `lengths` or of `response_mask` on one device may be relied on, other than what follows from the above.
Results may differ from a plain program's by a relative error of at most 0.0027.
Values may be sent and summed in bfloat16 or wider, within the bound.
A program may use at most 64 MiB of HBM per device.

v0:
```python
import jax
import jax.numpy as jnp
from jax import lax
from jax.sharding import PartitionSpec as P


def vocab_sums(states, targets, table, vocab_start):
    raw = lax.dot_general(
        states, table, (((1,), (1,)), ((), ())), preferred_element_type=jnp.float32
    )
    logits = 30.0 * jnp.tanh(raw / 30.0)
    expo = jnp.exp(logits)
    ident = vocab_start + lax.broadcasted_iota(jnp.int32, (1, table.shape[0]), 1)
    hit = jnp.where(ident == targets[:, None], logits, jnp.float32(0.0))
    return (jnp.sum(expo, axis=1), jnp.sum(expo * logits, axis=1), jnp.sum(hit, axis=1))


def on_device(hidden, norm_gain, embedding, target_ids, lengths, response_mask):
    seq_here, slots, width = hidden.shape
    rows = hidden.reshape(seq_here * slots, width).astype(jnp.float32)
    scale = lax.rsqrt(jnp.mean(rows * rows, axis=1, keepdims=True) + 1e-06)
    normed = (rows * scale * norm_gain[None, :]).astype(jnp.bfloat16)
    targets = target_ids.reshape(seq_here * slots)
    vocab_start = lax.axis_index(("req", "tp")) * embedding.shape[0]
    sums = vocab_sums(
        lax.all_gather(normed, ("req", "tp"), axis=0, tiled=True),
        lax.all_gather(targets, ("req", "tp"), axis=0, tiled=True),
        embedding,
        vocab_start,
    )
    gathered = tuple((new for new in sums))
    total, moment, picked = (
        lax.psum_scatter(gathered[0], ("req", "tp"), scatter_dimension=0, tiled=True),
        lax.psum_scatter(gathered[1], ("req", "tp"), scatter_dimension=0, tiled=True),
        lax.psum_scatter(gathered[2], ("req", "tp"), scatter_dimension=0, tiled=True),
    )
    lse = jnp.log(total)
    position = lax.axis_index("tp") * slots + lax.broadcasted_iota(jnp.int32, (seq_here, slots), 1)
    scored = (response_mask == 1) & (position < lengths[:, None])
    logprob = jnp.where(scored, (picked - lse).reshape(seq_here, slots), jnp.float32(0.0))
    entropy = jnp.where(scored, (lse - moment / total).reshape(seq_here, slots), jnp.float32(0.0))
    return (logprob, entropy)


def solution(mesh):
    return jax.shard_map(
        on_device,
        mesh=mesh,
        in_specs=(
            P("req", "tp", None),
            P(),
            P(("req", "tp"), None),
            P("req", "tp"),
            P("req"),
            P("req", "tp"),
        ),
        out_specs=(P("req", "tp"), P("req", "tp")),
        check_vma=False,
    )
```

profile of v0, /device:TPU:0, one launch (start us, length us, event | category | flops | bytes accessed | tf_op | source)
XLA Modules:
  0.0 119.0 jit_solution(6750184579432319236)
XLA Ops:
  7.2 0.0 copy-start
  7.2 0.0 all-gather.3.cloned.1.call-start
  7.2 1.1 fusion.3
  8.3 1.5 %fusion.5 = bf16[16,2048]{1,0:T(8,128)(2,1)} fusion(bf16[1,16,2048]{2,1,0:T(8,128)(2,1)} %param.6, f32[2048]{0:T(1024)} %param.7, f32[16]{0:T(128)S(1)} %add_rsqrt_fusion), kind=kLoop, calls=%fused_computation.11 | loop fusion | flops 131072 | bytes 139328 | tf_op jit(solution)/shard_map/convert_element_type | solution.py:22
  9.9 0.0 all-gather.3.cloned.1.call-update
  10.6 0.8 bitcast_dynamic-update-slice_fusion
  11.3 42.1 %all-reduce = s32[512]{0:T(512)S(1)} all-reduce(s32[512]{0:T(512)S(1)} %bitcast_dynamic-update-slice_fusion), channel_id=2, replica_groups=mesh['req'=16,'tp'=2] {'req','tp'}, use_global_device_ids=true, to_apply=%add | all-reduce | flops 512 | bytes 4096
  53.4 0.0 copy-start.1
  53.4 16.5 %all-gather.3.cloned.1.call-done = bf16[512,2048]{1,0:T(8,128)(2,1)} async-done(((bf16[16,2048]{1,0:T(8,128)(2,1)}), bf16[512,2048]{1,0:T(8,128)(2,1)}) %all-gather.3.cloned.1.call-update) | async-done | bytes 2097168 | tf_op jit(solution)/shard_map/all_gather | solution.py:26
  69.9 0.0 copy-done
  69.9 3.2 %fusion.2 = (f32[512]{0:T(512)S(1)}, f32[512]{0:T(512)S(1)}, f32[512]{0:T(512)S(1)}) fusion(s32[512]{0:T(512)S(1)} %all-reduce, s32[512]{0:T(512)S(1)} %iota_add_fusion, bf16[512,2048]{1,0:T(8,128)(2,1)} %all-gather.3.cloned.1.call-done, bf16[512,2048]{1,0:T(8,128)(2,1)S(1)} %copy-done), kind=kOutput, calls=%fused_computation.5 | convolution fusion | flops 1075837440 | bytes 4204544 | tf_op jit(solution)/shard_map/dot_general | solution.py:8
  73.1 38.5 %all-reduce.4 = (f32[512]{0:T(512)S(1)}, f32[512]{0:T(512)S(1)}, f32[512]{0:T(512)S(1)}) all-reduce(f32[512]{0:T(512)S(1)} %get-tuple-element.4, f32[512]{0:T(512)S(1)} %get-tuple-element.3, f32[512]{0:T(512)S(1)} %get-tuple-element.2), channel_id=3, replica_groups=mesh['req'=16,'tp'=2] {'req','tp'}, use_global_device_ids=true, to_apply=%region_2.3.clone | all-reduce | flops 1536 | bytes 12288
  111.6 0.0 copy-done.1
  111.6 0.6 bitcast_select_fusion
  (3 shorter events, 0.0 us)
Async XLA Ops:
  7.2 62.8 %copy-start = (bf16[512,2048]{1,0:T(8,128)(2,1)S(1)}, bf16[512,2048]{1,0:T(8,128)(2,1)}, u32[]{:S(2)}) copy-start(bf16[512,2048]{1,0:T(8,128)(2,1)} %param.8) | copy-start | bytes 6291460
  7.2 62.7 %all-gather.3.cloned.1.call-start = ((), (), s32[]{:S(2)}) async-start(), calls=%async_computation | async-start | bytes 2162688 | tf_op jit(solution)/shard_map/all_gather | solution.py:26
  53.4 58.2 %copy-start.1 = (s32[1,16]{1,0:T(1,128)S(1)}, s32[1,16]{1,0:T(1,128)}, u32[]{:S(2)}) copy-start(s32[1,16]{1,0:T(1,128)} %param.11) | copy-start | bytes 196
Sparse Core Ops, SparseCore 0:
  10.8 59.0 all-gather.2
where the time goes:
time: 119 us
  blocking collectives  80.6 us (68%)
  waiting for transfers between devices  16.5 us (14%)
  between operations  14.7 us (12%)
  other arithmetic  3.27 us (3%)
  matrix products  3.18 us (3%)
    unnamed x2, blocking collectives  80.6 us
    all_gather x1, waiting for transfers between devices, on_device(): lax.all_gather(normed, ('req', 'tp'), axis=0, tiled=True)  16.5 us
    dot_general x1, matrix products, vocab_sums(): lax.dot_general(states, table, (((1,), (1,)), ((), ())), preferred_elemen...  3.18 us
  transfers between devices with their start and end apart: 1, of which 1 were waited for; matrix products, arithmetic and copies ran while one was open for 1% of the time, Pallas kernels for 0%

commit v1 on v0

--- a/solution.py
+++ b/solution.py
@@ -1,7 +1,25 @@
+import functools
+
 import jax
 import jax.numpy as jnp
 from jax import lax
+from jax.experimental import pallas as pl
+from jax.experimental.pallas import tpu as pltpu
 from jax.sharding import PartitionSpec as P
+
+MESH = pl.DeviceIdType.MESH
+SPECS = dict(
+    in_specs=(
+        P("req", "tp", None),
+        P(),
+        P(("req", "tp"), None),
+        P("req", "tp"),
+        P("req"),
+        P("req", "tp"),
+    ),
+    out_specs=(P("req", "tp"), P("req", "tp")),
+    check_vma=False,
+)
 
 
 def vocab_sums(states, targets, table, vocab_start):
@@ -28,11 +46,8 @@
         embedding,
         vocab_start,
     )
-    gathered = tuple((new for new in sums))
     total, moment, picked = (
-        lax.psum_scatter(gathered[0], ("req", "tp"), scatter_dimension=0, tiled=True),
-        lax.psum_scatter(gathered[1], ("req", "tp"), scatter_dimension=0, tiled=True),
-        lax.psum_scatter(gathered[2], ("req", "tp"), scatter_dimension=0, tiled=True),
+        lax.psum_scatter(s, ("req", "tp"), scatter_dimension=0, tiled=True) for s in sums
     )
     lse = jnp.log(total)
     position = lax.axis_index("tp") * slots + lax.broadcasted_iota(jnp.int32, (seq_here, slots), 1)
@@ -42,18 +57,183 @@
     return (logprob, entropy)
 
 
+def J(b, a, area, dz):
+    return b * 16 + a * 8 + area * 4 + dz
+
+
+def kernel(slots, hidden_ref, gain_ref, target_ref, length_ref, mask_ref, emb_hbm,
+           lp_ref, ent_ref, emb, X, part, R, emb_sem, xs, xr, rs, rr):
+    width = hidden_ref.shape[1]
+    voc = emb.shape[0]
+    q, c = lax.axis_index("req"), lax.axis_index("tp")
+    x, y, z = q % 2, (q // 2) % 2, q // 4
+
+    def device(dz, fa, fb, core):
+        fx, fy = fa * (1 - c) + fb * c, fb * (1 - c) + fa * c
+        nx, ny = x + fx * (1 - 2 * x), y + fy * (1 - 2 * y)
+        nz = (z, z + 1 - 2 * (z % 2), z + 2 - 4 * (z // 2), 3 - z)[dz]
+        return (nz * 4 + ny * 2 + nx, core)
+
+    load = pltpu.make_async_copy(emb_hbm, emb, emb_sem)
+    load.start()
+    barrier = pltpu.get_barrier_semaphore()
+    near = [device(1, 0, 0, c), device(2, 0, 0, c), device(3, 0, 0, c),
+            device(0, 1, 0, c), device(0, 0, 1, c), device(0, 0, 0, 1 - c)]
+    for d in near:
+        pl.semaphore_signal(barrier, inc=1, device_id=d, device_id_type=MESH)
+
+    rows = hidden_ref[...].astype(jnp.float32)
+    scale = lax.rsqrt(jnp.mean(rows * rows, axis=1, keepdims=True) + 1e-06)
+    X[0:slots, 0:width] = (rows * scale * gain_ref[...]).astype(jnp.bfloat16)
+    tgt = jnp.broadcast_to(target_ref[...], (slots, slots))
+    eye = lax.broadcasted_iota(jnp.int32, (slots, slots), 0) == lax.broadcasted_iota(
+        jnp.int32, (slots, slots), 1)
+    tcol = jnp.sum(jnp.where(eye, tgt, 0).astype(jnp.float32), axis=1, keepdims=True)
+    high = jnp.floor(tcol * (1.0 / 256.0))
+    low = tcol - high * 256.0
+    lane = lax.broadcasted_iota(jnp.int32, (slots, 128), 1)
+    X[0:slots, width:width + 128] = jnp.where(
+        lane == 0, high, jnp.where(lane == 1, low, 0.0)).astype(jnp.bfloat16)
+    pl.semaphore_wait(barrier, len(near))
+
+    def block(slot):
+        return X.at[pl.ds(slot * slots, slots), :]
+
+    sends = []
+
+    def send(src, dst, dev):
+        copy = pltpu.make_async_remote_copy(
+            src_ref=block(src), dst_ref=block(dst), send_sem=xs.at[len(sends)],
+            recv_sem=xr.at[dst], device_id=dev, device_id_type=MESH)
+        copy.start()
+        sends.append(copy)
+
+    def arrived(slot):
+        pltpu.make_async_remote_copy(
+            src_ref=block(slot), dst_ref=block(slot), send_sem=xs.at[0],
+            recv_sem=xr.at[slot], device_id=near[5], device_id_type=MESH).wait_recv()
+
+    def forward(b, a, dz):
+        if b == 0 and a == 0:
+            send(J(0, 0, 0, dz), J(0, 1, 0, dz), near[3])
+        if b == 0:
+            send(J(0, a, 0, dz), J(1, a, 0, dz), near[4])
+        send(J(b, a, 0, dz), J(b, a, 1, dz), near[5])
+
+    def relay(b, a, dz):
+        arrived(J(b, a, 0, dz))
+        forward(b, a, dz)
+
+    start = ((q * 2 + c) * voc).astype(jnp.float32)
+    outs = []
+
+    def group(b, a):
+        for dz in range(4):
+            arrived(J(b, a, 1, dz))
+        base = J(b, a, 0, 0) * slots
+        g = b * 2 + a
+        toks = 8 * slots
+        pick = lax.broadcasted_iota(jnp.int32, (8, 128), 1)
+        pick = jnp.where(pick == 0, 256.0, jnp.where(pick == 1, 1.0, 0.0)).astype(jnp.bfloat16)
+        target = lax.dot_general(
+            pick, X[base:base + toks, width:width + 128], (((1,), (1,)), ((), ())),
+            preferred_element_type=jnp.float32)[0:1, :] - start
+        raw = lax.dot_general(
+            emb[...], X[base:base + toks, 0:width], (((1,), (1,)), ((), ())),
+            preferred_element_type=jnp.float32)
+        logits = 30.0 * jnp.tanh(raw / 30.0)
+        expo = jnp.exp(logits)
+        ident = lax.broadcasted_iota(jnp.int32, (voc, toks), 0).astype(jnp.float32)
+        part[g, 0:1, :] = jnp.sum(expo, axis=0, keepdims=True)
+        part[g, 1:2, :] = jnp.sum(expo * logits, axis=0, keepdims=True)
+        part[g, 2:3, :] = jnp.sum(jnp.where(ident == target, logits, 0.0), axis=0, keepdims=True)
+        part[g, 3:4, :] = jnp.zeros((1, toks), jnp.float32)
+        for area in (1, 0):
+            for dz in (3, 2, 1, 0):
+                slot = J(b, a, area, dz)
+                if slot == 0:
+                    continue
+                fa, fb = (a, b) if area == 0 else (b, a)
+                copy = pltpu.make_async_remote_copy(
+                    src_ref=part.at[g], dst_ref=R.at[slot], send_sem=rs.at[slot],
+                    recv_sem=rr.at[slot],
+                    device_id=device(dz, fa, fb, c if area == 0 else 1 - c),
+                    device_id_type=MESH)
+                copy.start()
+                outs.append(copy)
+
+    for dz in (3, 2, 1):
+        send(0, J(0, 0, 0, dz), near[dz - 1])
+    forward(0, 0, 0)
+    relay(0, 0, 1)
+    relay(0, 1, 0)
+    relay(0, 0, 2)
+    relay(0, 0, 3)
+    relay(1, 0, 0)
+    relay(0, 1, 1)
+    relay(0, 1, 2)
+    relay(0, 1, 3)
+    load.wait()
+    group(0, 0)
+    for dz in (1, 2, 3):
+        relay(1, 0, dz)
+    group(0, 1)
+    for dz in range(4):
+        relay(1, 1, dz)
+    group(1, 0)
+    group(1, 1)
+
+    for copy in outs:
+        copy.wait_recv()
+    home = lax.broadcasted_iota(jnp.int32, (4, 8 * slots), 1) // slots
+    acc = None
+    for k in range(8):
+        s = part[0] if k == 0 else R[k]
+        for g in range(1, 4):
+            s = s + R[g * 8 + k]
+        s = jnp.where(home == k, s, 0.0)
+        acc = s if acc is None else acc + s
+    for shift in (64, 32, 16):
+        acc = acc + pltpu.roll(acc, shift, 1)
+    total, moment, picked = (acc[i:i + 1, 0:slots] for i in range(3))
+    lse = jnp.log(total)
+    position = c * slots + lax.broadcasted_iota(jnp.int32, (1, slots), 1)
+    scored = (mask_ref[...] == 1) & (position < length_ref[0])
+    lp_ref[...] = jnp.where(scored, picked - lse, 0.0)
+    ent_ref[...] = jnp.where(scored, lse - moment / total, 0.0)
+    for copy in sends:
+        copy.wait_send()
+    for copy in outs:
+        copy.wait_send()
+
+
+def fused(hidden, norm_gain, embedding, target_ids, lengths, response_mask):
+    _, slots, width = hidden.shape
+    voc = embedding.shape[0]
+    vmem = pl.BlockSpec(memory_space=pltpu.VMEM)
+    out = jax.ShapeDtypeStruct((1, slots), jnp.float32)
+    return pl.pallas_call(
+        functools.partial(kernel, slots),
+        out_shape=(out, out),
+        in_specs=[vmem, vmem, vmem, pl.BlockSpec(memory_space=pltpu.SMEM), vmem,
+                  pl.BlockSpec(memory_space=pl.ANY)],
+        out_specs=(vmem, vmem),
+        scratch_shapes=[
+            pltpu.VMEM((voc, width), jnp.bfloat16),
+            pltpu.VMEM((32 * slots, width + 128), jnp.bfloat16),
+            pltpu.VMEM((4, 4, 8 * slots), jnp.float32),
+            pltpu.VMEM((32, 4, 8 * slots), jnp.float32),
+            pltpu.SemaphoreType.DMA,
+            pltpu.SemaphoreType.DMA((32,)),
+            pltpu.SemaphoreType.DMA((32,)),
+            pltpu.SemaphoreType.DMA((32,)),
+            pltpu.SemaphoreType.DMA((32,)),
+        ],
+        compiler_params=pltpu.CompilerParams(collective_id=0, has_side_effects=True),
+    )(hidden.reshape(slots, width), norm_gain.reshape(1, width), target_ids, lengths,
+      response_mask, embedding)
+
+
 def solution(mesh):
-    return jax.shard_map(
-        on_device,
-        mesh=mesh,
-        in_specs=(
-            P("req", "tp", None),
-            P(),
-            P(("req", "tp"), None),
-            P("req", "tp"),
-            P("req"),
-            P("req", "tp"),
-        ),
-        out_specs=(P("req", "tp"), P("req", "tp")),
-        check_vma=False,
-    )
+    body = fused if dict(mesh.shape) == {"req": 16, "tp": 2} else on_device
+    return jax.shard_map(body, mesh=mesh, **SPECS)

time: 119 us -> 34.8 us (0.29)
  blocking collectives: 80.6 us -> 0 us
  Pallas kernels: 0 us -> 31.1 us
  waiting for transfers between devices: 16.5 us -> 0 us
  between operations: 14.7 us -> 1.29 us
  other arithmetic: 3.27 us -> 0 us
  matrix products: 3.18 us -> 0 us
  local copies, waits for them, and re-layouts: 0.77 us -> 2.25 us
    unnamed x2 -> x0, blocking collectives: 80.6 us -> none
    pallas_call x0 -> x1, Pallas kernels: none -> 31.1 us  [fused(): pl.pallas_call(functools.partial(kernel, slots), out_shape=(out, out), in...]
    all_gather x1 -> x0, waiting for transfers between devices: 16.5 us -> none  [on_device(): lax.all_gather(normed, ('req', 'tp'), axis=0, tiled=True)]
    dot_general x1 -> x0, matrix products: 3.18 us -> none  [vocab_sums(): lax.dot_general(states, table, (((1,), (1,)), ((), ())), preferred_elemen...]
    convert_element_type x1 -> x0, other arithmetic: 1.55 us -> none  [on_device(): normed = (rows * scale * norm_gain[None, :]).astype(jnp.bfloat16)]
    unnamed x6 -> x2, local copies, waits for them, and re-layouts: 0.77 us -> 2.25 us
  transfers between devices with their start and end apart: 1 -> 0, of which waited for: 1 -> 0; matrix products, arithmetic and copies ran while one was open for 1% -> 0% of each run, Pallas kernels for 0% -> 0%
where the time goes in v1:
time: 34.8 us; the launch traced here: 34.6 us
  Pallas kernels  31.1 us (89%)
  local copies, waits for them, and re-layouts  2.25 us (6%)
  between operations  1.29 us (4%)
    pallas_call x1, Pallas kernels, fused(): pl.pallas_call(functools.partial(kernel, slots), out_shape=(out, out), in...  31.1 us
    unnamed x2, local copies, waits for them, and re-layouts  2.25 us

profile of v1, /device:TPU:0, one launch (start us, length us, event | category | flops | bytes accessed | tf_op | source)
XLA Modules:
  0.0 34.6 jit_solution(4885804781853191749)
XLA Ops:
  1.3 31.1 %shard_map.77 = (f32[1,16]{1,0:T(1,128)}, f32[1,16]{1,0:T(1,128)}) custom-call(bf16[16,2048]{1,0:T(8,128)(2,1)} %bitcast.2, f32[1,2048]{1,0:T(1,128)} %bitcast.3, s32[1,16]{1,0:T(1,128)} %target_ref.1, s32[1]{0:T(128)S(6)} %copy.10.length_ref, s32[1,16]{1,0:T(1,128)} %mask_ref.1, bf16[512,2048]{1,0:T(8,128)(2,1)} %emb_hbm.1), custom_call_target="tpu_custom_call" | custom-call | tf_op jit(solution)/shard_map/pallas_call | solution.py:215
  32.3 1.1 %copy.11 = f32[1,16]{1,0:T(1,128)} copy(f32[1,16]{1,0:T(1,128)} %get-tuple-element.4) | data formatting | bytes 128
  33.4 1.1 %copy.12 = f32[1,16]{1,0:T(1,128)} copy(f32[1,16]{1,0:T(1,128)} %get-tuple-element.5) | data formatting | bytes 128

commit v2 on v0

--- a/solution.py
+++ b/solution.py
@@ -1,7 +1,25 @@
+import functools
+
 import jax
 import jax.numpy as jnp
 from jax import lax
+from jax.experimental import pallas as pl
+from jax.experimental.pallas import tpu as pltpu
 from jax.sharding import PartitionSpec as P
+
+MESH = pl.DeviceIdType.MESH
+SPECS = dict(
+    in_specs=(
+        P("req", "tp", None),
+        P(),
+        P(("req", "tp"), None),
+        P("req", "tp"),
+        P("req"),
+        P("req", "tp"),
+    ),
+    out_specs=(P("req", "tp"), P("req", "tp")),
+    check_vma=False,
+)
 
 
 def vocab_sums(states, targets, table, vocab_start):
@@ -28,11 +46,8 @@
         embedding,
         vocab_start,
     )
-    gathered = tuple((new for new in sums))
     total, moment, picked = (
-        lax.psum_scatter(gathered[0], ("req", "tp"), scatter_dimension=0, tiled=True),
-        lax.psum_scatter(gathered[1], ("req", "tp"), scatter_dimension=0, tiled=True),
-        lax.psum_scatter(gathered[2], ("req", "tp"), scatter_dimension=0, tiled=True),
+        lax.psum_scatter(s, ("req", "tp"), scatter_dimension=0, tiled=True) for s in sums
     )
     lse = jnp.log(total)
     position = lax.axis_index("tp") * slots + lax.broadcasted_iota(jnp.int32, (seq_here, slots), 1)
@@ -42,18 +57,212 @@
     return (logprob, entropy)
 
 
+PARTS = 1
+RELAYED = ()
+
+
+def J(b, a, area, s):
+    return s * 8 + b * 4 + a * 2 + area
+
+
+def kernel(slots, hidden_hbm, gain_hbm, target_hbm, mask_hbm, length_hbm, emb_hbm, out_ref,
+           hidden, gain, target_row, mask, length, emb, X, part, R,
+           load_sem, z_sem, a_sem, b_sem, c_sem, p_sem, xr, rs, rr):
+    width = hidden.shape[1]
+    voc = emb.shape[0]
+    q, c = lax.axis_index("req"), lax.axis_index("tp")
+    x, y, z = q % 2, (q // 2) % 2, q // 4
+    order = (z, 1 + z % 2, 2 - 2 * (z % 2) + z // 2, 3 - 3 * (z // 2))
+
+    def device(nz, fa, fb, core):
+        fx, fy = fa * (1 - c) + fb * c, fb * (1 - c) + fa * c
+        nx, ny = x + fx * (1 - 2 * x), y + fy * (1 - 2 * y)
+        return (nz * 4 + ny * 2 + nx, core)
+
+    column = [device(order[i], 0, 0, c) for i in range(1, 4)]
+    a_side, b_side, partner = device(z, 1, 0, c), device(z, 0, 1, c), device(z, 0, 0, 1 - c)
+    diagonal = device(z, 1, 1, c)
+    near = column + [a_side, b_side, diagonal, partner]
+
+    barrier = pltpu.get_barrier_semaphore()
+
+    for d in near:
+        pl.semaphore_signal(barrier, inc=1, device_id=d, device_id_type=MESH)
+
+    loads = [pltpu.make_async_copy(src, dst, load_sem.at[i]) for i, (src, dst) in enumerate(
+        ((hidden_hbm, hidden), (gain_hbm, gain), (target_hbm, target_row), (mask_hbm, mask),
+         (length_hbm, length), (emb_hbm, emb)))]
+    for copy in loads:
+        copy.start()
+    for copy in loads[:3]:
+        copy.wait()
+    rows = hidden[...].astype(jnp.float32)
+    scale = lax.rsqrt(jnp.mean(rows * rows, axis=1, keepdims=True) + 1e-06)
+    own = pl.ds(pl.multiple_of(z * 8 * slots, slots), slots)
+    X[own, 0:width] = (rows * scale * gain[...]).astype(jnp.bfloat16)
+    tgt = jnp.broadcast_to(target_row[...], (slots, slots))
+    eye = lax.broadcasted_iota(jnp.int32, (slots, slots), 0) == lax.broadcasted_iota(
+        jnp.int32, (slots, slots), 1)
+    tcol = jnp.sum(jnp.where(eye, tgt, 0).astype(jnp.float32), axis=1, keepdims=True)
+    high = jnp.floor(tcol * (1.0 / 256.0))
+    low = tcol - high * 256.0
+    lane = lax.broadcasted_iota(jnp.int32, (slots, 128), 1)
+    X[own, width:width + 128] = jnp.where(
+        lane == 0, high, jnp.where(lane == 1, low, 0.0)).astype(jnp.bfloat16)
+    pl.semaphore_wait(barrier, len(near))
+
+    piece = slots // PARTS
+
+    def block(slot, h):
+        return X.at[pl.ds(pl.multiple_of(slot * slots + h * piece, piece), piece), :]
+
+    def copy_of(src, dst, h, send_sem, dev):
+        return pltpu.make_async_remote_copy(
+            src_ref=block(src, h), dst_ref=block(dst, h), send_sem=send_sem,
+            recv_sem=xr.at[dst, h], device_id=dev, device_id_type=MESH)
+
+    def copies(b, a, i, h):
+        s, here, out = order[i], J(b, a, 0, order[i]), []
+        if b + a + i == 0:
+            for n in (0, 1, 2):
+                out.append(copy_of(here, here, h, z_sem.at[n, h], column[n]))
+        if b + a == 0:
+            out.append(copy_of(here, J(0, 1, 0, s), h, a_sem.at[i, h], a_side))
+            out.append(copy_of(here, J(1, 0, 0, s), h, b_sem.at[i, h], b_side))
+            if i not in RELAYED:
+                out.append(copy_of(here, J(1, 1, 0, s), h, c_sem.at[i, h], diagonal))
+        if b == 0 and a == 1 and i in RELAYED:
+            out.append(copy_of(here, J(1, 1, 0, s), h, c_sem.at[i, h], b_side))
+        out.append(copy_of(here, J(b, a, 1, s), h, p_sem.at[i * 4 + b * 2 + a, h], partner))
+        return out
+
+    sends = []
+
+    def forward(b, a, i, h):
+        for copy in copies(b, a, i, h):
+            copy.start()
+            sends.append(copy)
+
+    def arrived(slot, h):
+        copy_of(slot, slot, h, p_sem.at[0, h], partner).wait_recv()
+
+    def relay(b, a, i):
+        for h in range(PARTS):
+            arrived(J(b, a, 0, order[i]), h)
+            forward(b, a, i, h)
+
+    start = ((q * 2 + c) * voc).astype(jnp.float32)
+    outs = []
+
+    def group(i):
+        for b in range(2):
+            for a in range(2):
+                for h in range(PARTS):
+                    arrived(J(b, a, 1, order[i]), h)
+        toks = 8 * slots
+        base = pl.multiple_of(order[i] * toks, toks)
+        pick = lax.broadcasted_iota(jnp.int32, (8, 128), 1)
+        pick = jnp.where(pick == 0, 256.0, jnp.where(pick == 1, 1.0, 0.0)).astype(jnp.bfloat16)
+        target = lax.dot_general(
+            pick, X[pl.ds(base, toks), width:width + 128], (((1,), (1,)), ((), ())),
+            preferred_element_type=jnp.float32)[0:1, :] - start
+        raw = lax.dot_general(
+            emb[...], X[pl.ds(base, toks), 0:width], (((1,), (1,)), ((), ())),
+            preferred_element_type=jnp.float32)
+        logits = 30.0 * jnp.tanh(raw / 30.0)
+        expo = jnp.exp(logits)
+        ident = lax.broadcasted_iota(jnp.int32, (voc, toks), 0).astype(jnp.float32)
+        part[i, 0:1, :] = jnp.sum(expo, axis=0, keepdims=True)
+        part[i, 1:2, :] = jnp.sum(expo * logits, axis=0, keepdims=True)
+        part[i, 2:3, :] = jnp.sum(jnp.where(ident == target, logits, 0.0), axis=0, keepdims=True)
+        part[i, 3:4, :] = jnp.zeros((1, toks), jnp.float32)
+        for k in range(7, -1, -1):
+            if i + k == 0:
+                continue
+            b, a, area = k // 4, k // 2 % 2, k % 2
+            fa, fb = (a, b) if area == 0 else (b, a)
+            copy = pltpu.make_async_remote_copy(
+                src_ref=part.at[i], dst_ref=R.at[z * 8 + k], send_sem=rs.at[i * 8 + k],
+                recv_sem=rr.at[z * 8 + k],
+                device_id=device(order[i], fa, fb, c if area == 0 else 1 - c),
+                device_id_type=MESH)
+            copy.start()
+            outs.append((copy, order[i] * 8 + k))
+
+    for h in range(PARTS):
+        forward(0, 0, 0, h)
+    relay(0, 0, 1)
+    relay(0, 1, 0)
+    relay(1, 0, 0)
+    relay(0, 0, 2)
+    relay(1, 1, 0)
+    relay(0, 0, 3)
+    for copy in loads[3:]:
+        copy.wait()
+    group(0)
+    for b, a in ((0, 1), (1, 0), (1, 1)):
+        relay(b, a, 1)
+    group(1)
+    for b, a in ((0, 1), (1, 0), (1, 1)):
+        relay(b, a, 2)
+    group(2)
+    for b, a in ((0, 1), (1, 0), (1, 1)):
+        relay(b, a, 3)
+    group(3)
+
+    for _, slot in outs:
+        pltpu.make_async_remote_copy(
+            src_ref=part.at[0], dst_ref=R.at[slot], send_sem=rs.at[0], recv_sem=rr.at[slot],
+            device_id=partner, device_id_type=MESH).wait_recv()
+    R[z * 8] = part[0]
+    home = lax.broadcasted_iota(jnp.int32, (4, 8 * slots), 1) // slots
+    acc = jnp.zeros((4, 8 * slots), jnp.float32)
+    for k in range(8):
+        acc = acc + jnp.where(home == k, (R[k] + R[8 + k]) + (R[16 + k] + R[24 + k]), 0.0)
+    for shift in (64, 32, 16):
+        acc = acc + pltpu.roll(acc, shift, 1)
+    total, moment, picked = (acc[i:i + 1, 0:slots] for i in range(3))
+    lse = jnp.log(total)
+    position = c * slots + lax.broadcasted_iota(jnp.int32, (1, slots), 1)
+    scored = (mask[...] == 1) & (position < length[0])
+    out_ref[0:1, :] = jnp.where(scored, picked - lse, 0.0)
+    out_ref[1:2, :] = jnp.where(scored, lse - moment / total, 0.0)
+
+    for copy in sends:
+        copy.wait_send()
+    for copy, _ in outs:
+        copy.wait_send()
+
+
+def fused(hidden, norm_gain, embedding, target_ids, lengths, response_mask):
+    _, slots, width = hidden.shape
+    voc = embedding.shape[0]
+    anywhere = pl.BlockSpec(memory_space=pl.ANY)
+    dma = pltpu.SemaphoreType.DMA
+    out = pl.pallas_call(
+        functools.partial(kernel, slots),
+        out_shape=jax.ShapeDtypeStruct((2, slots), jnp.float32),
+        in_specs=[anywhere] * 6,
+        out_specs=pl.BlockSpec(memory_space=pltpu.VMEM),
+        scratch_shapes=[
+            pltpu.VMEM((slots, width), jnp.bfloat16),
+            pltpu.VMEM((1, width), jnp.float32),
+            pltpu.VMEM((1, slots), jnp.int32),
+            pltpu.VMEM((1, slots), jnp.int32),
+            pltpu.SMEM((1,), jnp.int32),
+            pltpu.VMEM((voc, width), jnp.bfloat16),
+            pltpu.VMEM((32 * slots, width + 128), jnp.bfloat16),
+            pltpu.VMEM((4, 4, 8 * slots), jnp.float32),
+            pltpu.VMEM((32, 4, 8 * slots), jnp.float32),
+            dma((6,)), dma((3, PARTS)), dma((4, PARTS)), dma((4, PARTS)), dma((4, PARTS)),
+            dma((16, PARTS)), dma((32, PARTS)), dma((32,)), dma((32,)),
+        ],
+        compiler_params=pltpu.CompilerParams(collective_id=0, has_side_effects=True),
+    )(hidden.reshape(slots, width), norm_gain.reshape(1, width), target_ids, response_mask,
+      lengths, embedding)
+    return (out[0:1], out[1:2])
+
+
 def solution(mesh):
-    return jax.shard_map(
-        on_device,
-        mesh=mesh,
-        in_specs=(
-            P("req", "tp", None),
-            P(),
-            P(("req", "tp"), None),
-            P("req", "tp"),
-            P("req"),
-            P("req", "tp"),
-        ),
-        out_specs=(P("req", "tp"), P("req", "tp")),
-        check_vma=False,
-    )
+    body = fused if dict(mesh.shape) == {"req": 16, "tp": 2} else on_device
+    return jax.shard_map(body, mesh=mesh, **SPECS)

time: 119 us -> 32.6 us (0.27)
  blocking collectives: 80.6 us -> 0 us
  Pallas kernels: 0 us -> 29.9 us
  waiting for transfers between devices: 16.5 us -> 0 us
  between operations: 14.7 us -> 1.29 us
  other arithmetic: 3.27 us -> 0 us
  matrix products: 3.18 us -> 0 us
    unnamed x2 -> x0, blocking collectives: 80.6 us -> none
    pallas_call x0 -> x1, Pallas kernels: none -> 29.9 us  [fused(): pl.pallas_call(functools.partial(kernel, slots), out_shape=jax.ShapeDtype...]
    all_gather x1 -> x0, waiting for transfers between devices: 16.5 us -> none  [on_device(): lax.all_gather(normed, ('req', 'tp'), axis=0, tiled=True)]
    dot_general x1 -> x0, matrix products: 3.18 us -> none  [vocab_sums(): lax.dot_general(states, table, (((1,), (1,)), ((), ())), preferred_elemen...]
    convert_element_type x1 -> x0, other arithmetic: 1.55 us -> none  [on_device(): normed = (rows * scale * norm_gain[None, :]).astype(jnp.bfloat16)]
    slice x0 -> x1, local copies, waits for them, and re-layouts: none -> 1.25 us  [fused(): return (out[0:1], out[1:2])]
  transfers between devices with their start and end apart: 1 -> 0, of which waited for: 1 -> 0; matrix products, arithmetic and copies ran while one was open for 1% -> 0% of each run, Pallas kernels for 0% -> 0%
where the time goes in v2:
time: 32.6 us; the launch traced here: 32.4 us
  Pallas kernels  29.9 us (92%)
  between operations  1.29 us (4%)
  local copies, waits for them, and re-layouts  1.25 us (4%)
    pallas_call x1, Pallas kernels, fused(): pl.pallas_call(functools.partial(kernel, slots), out_shape=jax.ShapeDtype...  29.9 us
    slice x1, local copies, waits for them, and re-layouts, fused(): return (out[0:1], out[1:2])  1.25 us

profile of v2, /device:TPU:0, one launch (start us, length us, event | category | flops | bytes accessed | tf_op | source)
XLA Modules:
  0.0 32.4 jit_solution(4518189721516400743)
XLA Ops:
  1.3 29.9 %shard_map.77 = f32[2,16]{1,0:T(2,128)} custom-call(bf16[16,2048]{1,0:T(8,128)(2,1)} %bitcast.2, f32[1,2048]{1,0:T(1,128)} %bitcast.3, s32[1,16]{1,0:T(1,128)} %target_hbm.1, s32[1,16]{1,0:T(1,128)} %mask_hbm.1, s32[1]{0:T(128)S(6)} %copy.8.length_hbm, bf16[512,2048]{1,0:T(8,128)(2,1)} %emb_hbm.1), custom_call_target="tpu_custom_call" | custom-call | tf_op jit(solution)/shard_map/pallas_call | solution.py:242
  31.1 1.3 %fusion = (f32[1,16]{1,0:T(1,128)}, f32[1,16]{1,0:T(1,128)}) fusion(f32[2,16]{1,0:T(2,128)} %shard_map.77), kind=kLoop, calls=%fused_computation | loop fusion | bytes 256 | tf_op jit(solution)/shard_map/slice | solution.py:263

commit v3 on v2

--- a/solution.py
+++ b/solution.py
@@ -127,10 +127,10 @@
             for n in (0, 1, 2):
                 out.append(copy_of(here, here, h, z_sem.at[n, h], column[n]))
         if b + a == 0:
+            if i not in RELAYED:
+                out.append(copy_of(here, J(1, 1, 0, s), h, c_sem.at[i, h], diagonal))
             out.append(copy_of(here, J(0, 1, 0, s), h, a_sem.at[i, h], a_side))
             out.append(copy_of(here, J(1, 0, 0, s), h, b_sem.at[i, h], b_side))
-            if i not in RELAYED:
-                out.append(copy_of(here, J(1, 1, 0, s), h, c_sem.at[i, h], diagonal))
         if b == 0 and a == 1 and i in RELAYED:
             out.append(copy_of(here, J(1, 1, 0, s), h, c_sem.at[i, h], b_side))
         out.append(copy_of(here, J(b, a, 1, s), h, p_sem.at[i * 4 + b * 2 + a, h], partner))
@@ -200,16 +200,18 @@
     for copy in loads[3:]:
         copy.wait()
     group(0)
-    for b, a in ((0, 1), (1, 0), (1, 1)):
-        relay(b, a, 1)
+    relay(0, 1, 1)
+    relay(1, 0, 1)
+    relay(1, 1, 1)
+    relay(0, 1, 2)
+    relay(1, 0, 2)
+    relay(1, 1, 2)
     group(1)
-    for b, a in ((0, 1), (1, 0), (1, 1)):
-        relay(b, a, 2)
+    relay(0, 1, 3)
+    relay(1, 0, 3)
+    relay(1, 1, 3)
     group(2)
-    for b, a in ((0, 1), (1, 0), (1, 1)):
-        relay(b, a, 3)
     group(3)
-
     for _, slot in outs:
         pltpu.make_async_remote_copy(
             src_ref=part.at[0], dst_ref=R.at[slot], send_sem=rs.at[0], recv_sem=rr.at[slot],

time: 32.6 us -> 30.7 us (0.942)
  Pallas kernels: 29.9 us -> 28 us
    pallas_call x1, Pallas kernels: 29.9 us -> 28 us  [fused(): pl.pallas_call(functools.partial(kernel, slots), out_shape=jax.ShapeDtype...]
where the time goes in v3:
time: 30.7 us; the launch traced here: 30.5 us
  Pallas kernels  28 us (91%)
  between operations  1.29 us (4%)
  local copies, waits for them, and re-layouts  1.25 us (4%)
    pallas_call x1, Pallas kernels, fused(): pl.pallas_call(functools.partial(kernel, slots), out_shape=jax.ShapeDtype...  28 us
    slice x1, local copies, waits for them, and re-layouts, fused(): return (out[0:1], out[1:2])  1.25 us

profile of v3, /device:TPU:0, one launch (start us, length us, event | category | flops | bytes accessed | tf_op | source)
XLA Modules:
  0.0 30.5 jit_solution(3760609519269811371)
XLA Ops:
  1.3 28.0 %shard_map.77 = f32[2,16]{1,0:T(2,128)} custom-call(bf16[16,2048]{1,0:T(8,128)(2,1)} %bitcast.2, f32[1,2048]{1,0:T(1,128)} %bitcast.3, s32[1,16]{1,0:T(1,128)} %target_hbm.1, s32[1,16]{1,0:T(1,128)} %mask_hbm.1, s32[1]{0:T(128)S(6)} %copy.8.length_hbm, bf16[512,2048]{1,0:T(8,128)(2,1)} %emb_hbm.1), custom_call_target="tpu_custom_call" | custom-call | tf_op jit(solution)/shard_map/pallas_call | solution.py:244
  29.2 1.3 %fusion = (f32[1,16]{1,0:T(1,128)}, f32[1,16]{1,0:T(1,128)}) fusion(f32[2,16]{1,0:T(2,128)} %shard_map.77), kind=kLoop, calls=%fused_computation | loop fusion | bytes 256 | tf_op jit(solution)/shard_map/slice | solution.py:265
